TPU v7x, 256 devices: a whole 4x4x8 slice. The times are simulated.
256 devices in a mesh: section: 8 (over z_hi, core), tp: 32 (over z_lo, x, y).
Axes of the slice: x: 4, y: 4, z: 8 (z_hi: 4, z_lo: 2; z = z_hi * 2 + z_lo), core: 2. Of those that a mesh axis runs over, the one named last changes fastest.
Arguments:
- start_tokens: bfloat16 [2, 32, 8192], P(None, None, 'tp'), may hold values from -6 to 6
- target_weight: bfloat16 [8, 8192, 8192], P('section', None, 'tp'), may hold values from -0.0625 to 0.0625
- online_weight: bfloat16 [8, 8192, 8192], P('section', 'tp'), may hold values from -0.0625 to 0.0625
- head_weight: bfloat16 [8192, 256], P('tp'), may hold values from -0.0625 to 0.0625
- reward: float32 [2, 32], P(None, 'section'), may hold values from -6 to 6
- action_bin: int32 [2, 32], P(None, 'section'), may hold values from 0 to 255
Outputs:
- target_value: float32 [2, 32], P(None, 'section')
- q_taken: float32 [2, 32], P(None, 'section')
All inputs are finite; a program needn't handle non-finite values.
Results may differ from a plain program's by a relative error of at most 0.018.
Values may be sent and summed in bfloat16 or wider, within the bound.
A program may use at most 64 MiB of HBM per device.

v0:
```python
import jax
import jax.numpy as jnp
from jax import lax
from jax.sharding import PartitionSpec as P


def shifted(block, axis, distance):
    devices = range(lax.axis_size(axis))
    route = [(i - distance, i) for i in devices if i - distance in devices]
    return lax.ppermute(block, axis, route)


def from_root(value, axis, source):
    kept = jnp.where(lax.axis_index(axis) == source, value, 0).astype(value.dtype)
    return lax.psum(kept, axis)


def per_device(start_tokens, target_weight, online_weight, head_weight, reward, action_bin):
    moved = lax.all_to_all(online_weight, "tp", split_axis=2, concat_axis=1, tiled=True)
    blended = (0.25 * moved.astype(jnp.float32) + 0.75 * target_weight.astype(jnp.float32)).astype(
        jnp.bfloat16
    )[0]
    sections = lax.axis_size("section")
    position = lax.axis_index("section")
    micro = start_tokens.shape[0]
    finished = jnp.zeros(start_tokens.shape, jnp.bfloat16)
    incoming = jnp.zeros(start_tokens.shape[1:], jnp.bfloat16)

    def advance(tick, carry):
        incoming, finished = carry
        fresh = lax.dynamic_index_in_dim(
            start_tokens, jnp.minimum(tick, micro - 1), 0, keepdims=False
        )
        source = jnp.where(position == 0, fresh, incoming)
        local = source.astype(jnp.float32)
        whole = lax.all_gather(source, "tp", axis=1, tiled=True)
        wide = whole.astype(jnp.float32)
        normed = (wide * lax.rsqrt(jnp.mean(wide * wide, axis=1, keepdims=True) + 1e-06)).astype(
            jnp.bfloat16
        )
        result = (local + jnp.dot(normed, blended, preferred_element_type=jnp.float32)).astype(
            jnp.bfloat16
        )
        slot = tick - (sections - 1)
        keep = jnp.logical_and(position == sections - 1, slot >= 0)
        placed = lax.dynamic_update_index_in_dim(finished, result, jnp.clip(slot, 0, micro - 1), 0)
        finished = jnp.where(keep, placed, finished)
        incoming = shifted(result, "section", 1)
        return (incoming, finished)

    incoming, finished = lax.fori_loop(0, micro + sections - 1, advance, (incoming, finished))
    outputs = from_root(finished, "section", sections - 1)
    share_rows = reward.shape[1]
    mine = lax.dynamic_slice_in_dim(outputs, position * share_rows, share_rows, 1)
    mine = mine.reshape(micro * share_rows, mine.shape[2])
    partial_value = jnp.dot(mine, head_weight, preferred_element_type=jnp.float32)
    actions = action_bin.reshape(micro * share_rows, 1)
    values = lax.psum(partial_value, "tp")
    best = jnp.max(values, axis=1)
    chosen = (jnp.arange(values.shape[1], dtype=jnp.int32)[None, :] == actions).astype(jnp.float32)
    taken = jnp.sum(values * chosen, axis=1)
    best = best.reshape(micro, share_rows)
    taken = taken.reshape(micro, share_rows)
    return (reward + 0.98 * best, taken)


def solution(mesh):
    in_specs = (
        P(None, None, "tp"),
        P("section", None, "tp"),
        P("section", "tp", None),
        P("tp", None),
        P(None, "section"),
        P(None, "section"),
    )
    out_specs = (P(None, "section"), P(None, "section"))
    return jax.shard_map(
        per_device, mesh=mesh, in_specs=in_specs, out_specs=out_specs, check_vma=False
    )
```

profile of v0, /device:TPU:136, one launch (start us, length us, event | category | flops | bytes accessed | tf_op | source)
XLA Modules:
  0.0 1105.1 jit_solution(2322913025078302848)
XLA Ops:
  0.6 17.9 %copy.9 = bf16[1,256,8192]{1,0,2:T(2,128)(2,1)} copy(bf16[1,256,8192]{2,1,0:T(8,128)(2,1)} %param.10) | data formatting | bytes 8388608 | tf_op args[2]
  19.0 43.5 %reduce = bf16[8192,256]{1,0:T(8,128)(2,1)} reduce(bf16[8192,1,256]{2,1,0:T(2,128)(2,1)} %bitcast.27, bf16[]{:T(256)} %broadcast.66), dimensions={1}, to_apply=%bitcast.14.reduce_sub_computation | reduce | bytes 8388610
  62.5 6.9 reshape.50
  69.5 8.0 all-to-all-start
  77.6 50.6 %all-to-all-done = bf16[32,2,32768]{2,1,0:T(2,128)(2,1)} async-done(((bf16[32,2,32768]{2,1,0:T(2,128)(2,1)}), bf16[32,2,32768]{2,1,0:T(2,128)(2,1)}, u32[]{:S(2)}, u32[]{:S(2)}) %all-to-all-start) | async-done | bytes 4194336 | tf_op jit(solution)/shard_map/all_to_all | solution.py:19
  128.2 19.8 %reshape.51 = bf16[8192,1,256]{2,1,0:T(2,128)(2,1)} reshape(bf16[32,2,32768]{2,1,0:T(2,128)(2,1)} %all-to-all-done) | data formatting | bytes 8388608
  148.0 10.9 convert_multiply_fusion.2
  158.8 19.2 %copy.10 = f32[1,32,256,256]{3,2,1,0:T(8,128)} copy(f32[1,32,256,256]{2,0,3,1:T(1,128)} %bitcast.28) | data formatting | bytes 16777216 | tf_op jit(solution)/shard_map/mul | solution.py:20
  178.0 7.5 fusion.6
  185.6 810.7 %while.17 = (s32[]{:T(128)}, bf16[32,256]{1,0:T(8,128)(2,1)S(1)}, bf16[2,32,256]{2,1,0:T(8,128)(2,1)S(1)}, pred[]{:T(512)}, bf16[2,32,256]{2,1,0:T(8,128)(2,1)S(...) while((s32[]{:T(128)}, bf16[32,256]{1,0:T(8,128)(2,1)S(1)}, ...), condition=%wide.region_2.3_spmd, body=%wide.region_0.2_spmd.sunk | while | flops 135831600 | bytes 5964925 | solution.py:51
  185.6 80.7 %all_gather.11 = bf16[32,8192]{1,0:T(8,128)(2,1)S(1)} all-gather(bf16[32,256]{1,0:T(8,128)(2,1)S(1)} %bitcast_select_fusion.3), channel_id=1, replica_groups=mesh['section'=8,'tp'=32] {'tp'}, dimensions={1}, use_global_device_ids=true | all-gather | bytes 540672 | tf_op jit(solution)/shard_map/while/body/eval_jaxpr/all_gather | solution.py:36
  271.5 5.2 collective-permute-done
  276.8 83.2 %all_gather.11 = bf16[32,8192]{1,0:T(8,128)(2,1)S(1)} all-gather(bf16[32,256]{1,0:T(8,128)(2,1)S(1)} %bitcast_select_fusion.3), channel_id=1, replica_groups=mesh['section'=8,'tp'=32] {'tp'}, dimensions={1}, use_global_device_ids=true | all-gather | bytes 540672 | tf_op jit(solution)/shard_map/while/body/eval_jaxpr/all_gather | solution.py:36
  365.2 5.2 collective-permute-done
  370.5 78.1 %all_gather.11 = bf16[32,8192]{1,0:T(8,128)(2,1)S(1)} all-gather(bf16[32,256]{1,0:T(8,128)(2,1)S(1)} %bitcast_select_fusion.3), channel_id=1, replica_groups=mesh['section'=8,'tp'=32] {'tp'}, dimensions={1}, use_global_device_ids=true | all-gather | bytes 540672 | tf_op jit(solution)/shard_map/while/body/eval_jaxpr/all_gather | solution.py:36
  459.1 80.0 %all_gather.11 = bf16[32,8192]{1,0:T(8,128)(2,1)S(1)} all-gather(bf16[32,256]{1,0:T(8,128)(2,1)S(1)} %bitcast_select_fusion.3), channel_id=1, replica_groups=mesh['section'=8,'tp'=32] {'tp'}, dimensions={1}, use_global_device_ids=true | all-gather | bytes 540672 | tf_op jit(solution)/shard_map/while/body/eval_jaxpr/all_gather | solution.py:36
  549.5 78.2 %all_gather.11 = bf16[32,8192]{1,0:T(8,128)(2,1)S(1)} all-gather(bf16[32,256]{1,0:T(8,128)(2,1)S(1)} %bitcast_select_fusion.3), channel_id=1, replica_groups=mesh['section'=8,'tp'=32] {'tp'}, dimensions={1}, use_global_device_ids=true | all-gather | bytes 540672 | tf_op jit(solution)/shard_map/while/body/eval_jaxpr/all_gather | solution.py:36
  638.2 79.9 %all_gather.11 = bf16[32,8192]{1,0:T(8,128)(2,1)S(1)} all-gather(bf16[32,256]{1,0:T(8,128)(2,1)S(1)} %bitcast_select_fusion.3), channel_id=1, replica_groups=mesh['section'=8,'tp'=32] {'tp'}, dimensions={1}, use_global_device_ids=true | all-gather | bytes 540672 | tf_op jit(solution)/shard_map/while/body/eval_jaxpr/all_gather | solution.py:36
  728.6 78.1 %all_gather.11 = bf16[32,8192]{1,0:T(8,128)(2,1)S(1)} all-gather(bf16[32,256]{1,0:T(8,128)(2,1)S(1)} %bitcast_select_fusion.3), channel_id=1, replica_groups=mesh['section'=8,'tp'=32] {'tp'}, dimensions={1}, use_global_device_ids=true | all-gather | bytes 540672 | tf_op jit(solution)/shard_map/while/body/eval_jaxpr/all_gather | solution.py:36
  812.0 5.2 collective-permute-done
  817.2 80.0 %all_gather.11 = bf16[32,8192]{1,0:T(8,128)(2,1)S(1)} all-gather(bf16[32,256]{1,0:T(8,128)(2,1)S(1)} %bitcast_select_fusion.3), channel_id=1, replica_groups=mesh['section'=8,'tp'=32] {'tp'}, dimensions={1}, use_global_device_ids=true | all-gather | bytes 540672 | tf_op jit(solution)/shard_map/while/body/eval_jaxpr/all_gather | solution.py:36
  907.7 78.0 %all_gather.11 = bf16[32,8192]{1,0:T(8,128)(2,1)S(1)} all-gather(bf16[32,256]{1,0:T(8,128)(2,1)S(1)} %bitcast_select_fusion.3), channel_id=1, replica_groups=mesh['section'=8,'tp'=32] {'tp'}, dimensions={1}, use_global_device_ids=true | all-gather | bytes 540672 | tf_op jit(solution)/shard_map/while/body/eval_jaxpr/all_gather | solution.py:36
  996.3 27.2 %psum.14 = bf16[2,32,256]{2,1,0:T(8,128)(2,1)S(1)} all-reduce(bf16[2,32,256]{2,1,0:T(8,128)(2,1)S(1)} %broadcast_select_fusion), channel_id=1, replica_groups=mesh['section'=8,'tp'=32] {'section'}, use_global_device_ids=true, to_apply=%region_3.4 | all-reduce | flops 16384 | bytes 65536 | tf_op jit(solution)/shard_map/psum | solution.py:15
  1023.7 80.0 %psum.15 = f32[8,256]{1,0:T(8,128)S(1)} all-reduce(f32[8,256]{1,0:T(8,128)S(1)} %fusion.7), channel_id=1, replica_groups=mesh['section'=8,'tp'=32] {'tp'}, use_global_device_ids=true, to_apply=%region_4.5 | all-reduce | flops 2048 | bytes 16384 | tf_op jit(solution)/shard_map/psum | solution.py:58
  (72 shorter events, 80.8 us)
Async XLA Ops:
  0.6 1022.9 %copy-start = (bf16[256,256]{1,0:T(8,128)(2,1)S(1)}, bf16[256,256]{1,0:T(8,128)(2,1)}, u32[]{:S(2)}) copy-start(bf16[256,256]{1,0:T(8,128)(2,1)} %param.11) | copy-start | bytes 393220
  62.5 15.0 %copy-start.3 = (s32[2,4]{1,0:T(2,128)S(1)}, s32[2,4]{1,0:T(2,128)}, u32[]{:S(2)}) copy-start(s32[2,4]{1,0:T(2,128)} %param.13) | copy-start | bytes 100
  69.5 58.7 %all-to-all-start = ((bf16[32,2,32768]{2,1,0:T(2,128)(2,1)}), bf16[32,2,32768]{2,1,0:T(2,128)(2,1)}, u32[]{:S(2)}, u32[]{:S(2)}) async-start(bf16[32,2,32768]{2,1,0:T(2,128)(2,1)} %reshape.50), calls=%async_computation | async-start | bytes 8388608 | tf_op jit(solution)/shard_map/all_to_all | solution.py:19
  178.0 7.5 copy-start.1
  185.6 919.0 %copy-start.2 = (f32[2,4]{1,0:T(2,128)S(1)}, f32[2,4]{1,0:T(2,128)}, u32[]{:S(2)}) copy-start(f32[2,4]{1,0:T(2,128)} %param.12) | copy-start | bytes 100
  269.6 7.2 collective-permute-start
  363.3 7.2 collective-permute-start
  451.9 7.2 collective-permute-start
  542.3 7.2 collective-permute-start
  631.0 7.2 collective-permute-start
  721.5 7.2 collective-permute-start
  810.0 7.2 collective-permute-start
  900.6 7.2 collective-permute-start
  989.1 7.2 collective-permute-start
where the time goes:
time: 1110 us
  blocking collectives  823 us (74%)
  waiting for transfers between devices  97.7 us (9%)
  local copies, waits for them, and re-layouts  65.1 us (6%)
  other arithmetic  64.9 us (6%)
  matrix products  27.7 us (2%)
  starting transfers between devices  25.3 us (2%)
    all_gather x9, blocking collectives, advance(): whole = lax.all_gather(source, 'tp', axis=1, tiled=True)  716 us
    psum x1, blocking collectives, per_device(): values = lax.psum(partial_value, 'tp')  80 us
    all_to_all x1, waiting for transfers between devices, per_device(): lax.all_to_all(online_weight, 'tp', split_axis=2, concat_axis=1, tiled=True)  50.6 us
    ppermute x9, waiting for transfers between devices, shifted(): return lax.ppermute(block, axis, route)  47.1 us
    unnamed x12, local copies, waits for them, and re-layouts  45.1 us
    unnamed x1, other arithmetic  43.5 us
    dot_general x9, matrix products, advance(): jnp.dot(normed, blended, preferred_element_type=jnp.float32)  27.6 us
    psum x1, blocking collectives, from_root(): return lax.psum(kept, axis)  27.2 us
  transfers between devices with their start and end apart: 10, of which 10 were waited for; matrix products, arithmetic and copies ran while one was open for 0% of the time, Pallas kernels for 0%

commit v1 on v0

--- a/solution.py
+++ b/solution.py
@@ -2,6 +2,13 @@
 import jax.numpy as jnp
 from jax import lax
 from jax.sharding import PartitionSpec as P
+
+
+def gather_over(x, axis, along):
+    size = lax.axis_size(axis)
+    blocks = jnp.stack([x for _ in range(size)])
+    blocks = lax.all_to_all(blocks, axis, split_axis=0, concat_axis=0)
+    return jnp.concatenate(blocks, axis=along)
 
 
 def shifted(block, axis, distance):
@@ -33,7 +40,7 @@
         )
         source = jnp.where(position == 0, fresh, incoming)
         local = source.astype(jnp.float32)
-        whole = lax.all_gather(source, "tp", axis=1, tiled=True)
+        whole = gather_over(source, "tp", 1)
         wide = whole.astype(jnp.float32)
         normed = (wide * lax.rsqrt(jnp.mean(wide * wide, axis=1, keepdims=True) + 1e-06)).astype(
             jnp.bfloat16

time: 1110 us -> 540 us (0.49)
  blocking collectives: 823 us -> 106 us
  waiting for transfers between devices: 97.7 us -> 179 us
  starting transfers between devices: 25.3 us -> 79.9 us
    all_gather x9 -> x0, blocking collectives: 716 us -> none  [advance(): whole = lax.all_gather(source, 'tp', axis=1, tiled=True)]
    all_to_all x0 -> x9, waiting for transfers between devices: none -> 81.6 us  [gather_over(): blocks = lax.all_to_all(blocks, axis, split_axis=0, concat_axis=0)]
    all_to_all x0 -> x9, starting transfers between devices: none -> 54.6 us  [gather_over(): blocks = lax.all_to_all(blocks, axis, split_axis=0, concat_axis=0)]
  transfers between devices with their start and end apart: 10 -> 19, of which waited for: 10 -> 19; matrix products, arithmetic and copies ran while one was open for 0% -> 0% of each run, Pallas kernels for 0% -> 0%
where the time goes in v1:
time: 540 us; the launch traced here: 534 us
  waiting for transfers between devices  179 us (33%)
  blocking collectives  106 us (20%)
  starting transfers between devices  79.9 us (15%)
  local copies, waits for them, and re-layouts  73.5 us (14%)
  other arithmetic  65.9 us (12%)
  matrix products  27.8 us (5%)
    all_to_all x9, waiting for transfers between devices, gather_over(): blocks = lax.all_to_all(blocks, axis, split_axis=0, concat_axis=0)  81.6 us
    psum x1, blocking collectives, per_device(): values = lax.psum(partial_value, 'tp')  79.3 us
    all_to_all x9, starting transfers between devices, gather_over(): blocks = lax.all_to_all(blocks, axis, split_axis=0, concat_axis=0)  54.6 us
    all_to_all x1, waiting for transfers between devices, per_device(): lax.all_to_all(online_weight, 'tp', split_axis=2, concat_axis=1, tiled=True)  50.6 us
    ppermute x9, waiting for transfers between devices, shifted(): return lax.ppermute(block, axis, route)  47.1 us
    unnamed x12, local copies, waits for them, and re-layouts  45.1 us
    unnamed x1, other arithmetic  43.5 us
    dot_general x9, matrix products, advance(): jnp.dot(normed, blended, preferred_element_type=jnp.float32)  27.7 us
  transfers between devices with their start and end apart: 19, of which 19 were waited for; matrix products, arithmetic and copies ran while one was open for 0% of the time, Pallas kernels for 0%

profile of v1, /device:TPU:136, one launch (start us, length us, event | category | flops | bytes accessed | tf_op | source)
XLA Modules:
  0.0 534.2 jit_solution(8261143864675311437)
XLA Ops:
  0.6 17.9 %copy.11 = bf16[1,256,8192]{1,0,2:T(2,128)(2,1)} copy(bf16[1,256,8192]{2,1,0:T(8,128)(2,1)} %param.10) | data formatting | bytes 8388608 | tf_op args[2]
  19.0 43.5 %reduce.2 = bf16[8192,256]{1,0:T(8,128)(2,1)} reduce(bf16[8192,1,256]{2,1,0:T(2,128)(2,1)} %bitcast.36, bf16[]{:T(256)} %broadcast.73), dimensions={1}, to_apply=%bitcast.18.reduce_sub_computation | reduce | bytes 8388610
  62.5 6.9 %reshape.71 = bf16[32,2,32768]{2,1,0:T(2,128)(2,1)} reshape(bf16[8192,256]{1,0:T(8,128)(2,1)} %reduce.2) | data formatting | bytes 8388608
  69.5 8.0 %all-to-all-start.1 = ((bf16[32,2,32768]{2,1,0:T(2,128)(2,1)}), bf16[32,2,32768]{2,1,0:T(2,128)(2,1)}, u32[]{:S(2)}, u32[]{:S(2)}) async-start(bf16[32,2,32768]{2,1,0:T(2,128)(2,1)} %reshape.71), calls=%async_computation.1 | async-start | bytes 8388608 | tf_op jit(solution)/shard_map/all_to_all | solution.py:26
  77.6 50.6 %all-to-all-done.1 = bf16[32,2,32768]{2,1,0:T(2,128)(2,1)} async-done(((bf16[32,2,32768]{2,1,0:T(2,128)(2,1)}), bf16[32,2,32768]{2,1,0:T(2,128)(2,1)}, u32[]{:S(2)}, u32[]{:S(2)}) %all-to-all-start.1) | async-done | bytes 4194336 | tf_op jit(solution)/shard_map/all_to_all | solution.py:26
  128.2 19.8 %reshape.72 = bf16[8192,1,256]{2,1,0:T(2,128)(2,1)} reshape(bf16[32,2,32768]{2,1,0:T(2,128)(2,1)} %all-to-all-done.1) | data formatting | bytes 8388608
  148.0 10.9 %convert_multiply_fusion.1 = f32[1,256,8192]{1,0,2:T(1,128)} fusion(bf16[8192,1,256]{2,1,0:T(2,128)(2,1)} %reshape.72), kind=kLoop, calls=%fused_computation.13 | loop fusion | flops 4194304 | bytes 12582912 | tf_op jit(solution)/shard_map/mul | solution.py:27
  158.8 19.2 %copy.12 = f32[1,32,256,256]{3,2,1,0:T(8,128)} copy(f32[1,32,256,256]{2,0,3,1:T(1,128)} %bitcast.37) | data formatting | bytes 16777216 | tf_op jit(solution)/shard_map/mul | solution.py:27
  178.0 7.5 %fusion.4 = bf16[1,8192,256]{2,1,0:T(8,128)(2,1)} fusion(f32[1,32,256,256]{3,2,1,0:T(8,128)} %copy.12, bf16[1,8192,256]{2,1,0:T(8,128)(2,1)} %param.9), kind=kLoop, calls=%fused_computation.12 | loop fusion | flops 8388608 | bytes 16777216 | tf_op jit(solution)/shard_map/convert_element_type | solution.py:27
  185.6 240.5 %while.17 = (s32[]{:T(128)}, bf16[32,256]{1,0:T(8,128)(2,1)S(1)}, bf16[2,32,256]{2,1,0:T(8,128)(2,1)S(1)}, pred[]{:T(512)}, bf16[2,32,256]{2,1,0:T(8,128)(2,1)S(...) while((s32[]{:T(128)}, bf16[32,256]{1,0:T(8,128)(2,1)S(1)}, ...), condition=%wide.region_2.3_spmd, body=%wide.region_0.2_spmd.sunk | while | flops 135831600 | bytes 11732125 | solution.py:58
  186.5 11.4 %all-to-all-start = ((bf16[32,32,256]{2,1,0:T(8,128)(2,1)}), bf16[32,32,256]{2,1,0:T(8,128)(2,1)S(1)}, u32[]{:S(2)}, u32[]{:S(2)}) async-start(bf16[32,32,256]{2,1,0:T(8,128)(2,1)} %stack.7), calls=%async_computation | async-start | bytes 1048576 | tf_op jit(solution)/shard_map/while/body/eval_jaxpr/all_to_all | solution.py:10
  197.9 10.5 %all-to-all-done = bf16[32,32,256]{2,1,0:T(8,128)(2,1)S(1)} async-done(((bf16[32,32,256]{2,1,0:T(8,128)(2,1)}), bf16[32,32,256]{2,1,0:T(8,128)(2,1)S(1)}, u32[]{:S(2)}, u32[]{:S(2)}) %all-to-all-start) | async-done | bytes 524320 | tf_op jit(solution)/shard_map/while/body/eval_jaxpr/all_to_all | solution.py:10
  219.9 5.4 %all-to-all-start = ((bf16[32,32,256]{2,1,0:T(8,128)(2,1)}), bf16[32,32,256]{2,1,0:T(8,128)(2,1)S(1)}, u32[]{:S(2)}, u32[]{:S(2)}) async-start(bf16[32,32,256]{2,1,0:T(8,128)(2,1)} %stack.7), calls=%async_computation | async-start | bytes 1048576 | tf_op jit(solution)/shard_map/while/body/eval_jaxpr/all_to_all | solution.py:10
  225.3 8.9 %all-to-all-done = bf16[32,32,256]{2,1,0:T(8,128)(2,1)S(1)} async-done(((bf16[32,32,256]{2,1,0:T(8,128)(2,1)}), bf16[32,32,256]{2,1,0:T(8,128)(2,1)S(1)}, u32[]{:S(2)}, u32[]{:S(2)}) %all-to-all-start) | async-done | bytes 524320 | tf_op jit(solution)/shard_map/while/body/eval_jaxpr/all_to_all | solution.py:10
  245.8 5.4 %all-to-all-start = ((bf16[32,32,256]{2,1,0:T(8,128)(2,1)}), bf16[32,32,256]{2,1,0:T(8,128)(2,1)S(1)}, u32[]{:S(2)}, u32[]{:S(2)}) async-start(bf16[32,32,256]{2,1,0:T(8,128)(2,1)} %stack.7), calls=%async_computation | async-start | bytes 1048576 | tf_op jit(solution)/shard_map/while/body/eval_jaxpr/all_to_all | solution.py:10
  251.2 8.9 %all-to-all-done = bf16[32,32,256]{2,1,0:T(8,128)(2,1)S(1)} async-done(((bf16[32,32,256]{2,1,0:T(8,128)(2,1)}), bf16[32,32,256]{2,1,0:T(8,128)(2,1)S(1)}, u32[]{:S(2)}, u32[]{:S(2)}) %all-to-all-start) | async-done | bytes 524320 | tf_op jit(solution)/shard_map/while/body/eval_jaxpr/all_to_all | solution.py:10
  277.1 8.9 %all-to-all-done = bf16[32,32,256]{2,1,0:T(8,128)(2,1)S(1)} async-done(((bf16[32,32,256]{2,1,0:T(8,128)(2,1)}), bf16[32,32,256]{2,1,0:T(8,128)(2,1)S(1)}, u32[]{:S(2)}, u32[]{:S(2)}) %all-to-all-start) | async-done | bytes 524320 | tf_op jit(solution)/shard_map/while/body/eval_jaxpr/all_to_all | solution.py:10
  303.0 8.9 %all-to-all-done = bf16[32,32,256]{2,1,0:T(8,128)(2,1)S(1)} async-done(((bf16[32,32,256]{2,1,0:T(8,128)(2,1)}), bf16[32,32,256]{2,1,0:T(8,128)(2,1)S(1)}, u32[]{:S(2)}, u32[]{:S(2)}) %all-to-all-start) | async-done | bytes 524320 | tf_op jit(solution)/shard_map/while/body/eval_jaxpr/all_to_all | solution.py:10
  328.9 8.9 %all-to-all-done = bf16[32,32,256]{2,1,0:T(8,128)(2,1)S(1)} async-done(((bf16[32,32,256]{2,1,0:T(8,128)(2,1)}), bf16[32,32,256]{2,1,0:T(8,128)(2,1)S(1)}, u32[]{:S(2)}, u32[]{:S(2)}) %all-to-all-start) | async-done | bytes 524320 | tf_op jit(solution)/shard_map/while/body/eval_jaxpr/all_to_all | solution.py:10
  354.7 8.9 %all-to-all-done = bf16[32,32,256]{2,1,0:T(8,128)(2,1)S(1)} async-done(((bf16[32,32,256]{2,1,0:T(8,128)(2,1)}), bf16[32,32,256]{2,1,0:T(8,128)(2,1)S(1)}, u32[]{:S(2)}, u32[]{:S(2)}) %all-to-all-start) | async-done | bytes 524320 | tf_op jit(solution)/shard_map/while/body/eval_jaxpr/all_to_all | solution.py:10
  380.6 8.9 %all-to-all-done = bf16[32,32,256]{2,1,0:T(8,128)(2,1)S(1)} async-done(((bf16[32,32,256]{2,1,0:T(8,128)(2,1)}), bf16[32,32,256]{2,1,0:T(8,128)(2,1)S(1)}, u32[]{:S(2)}, u32[]{:S(2)}) %all-to-all-start) | async-done | bytes 524320 | tf_op jit(solution)/shard_map/while/body/eval_jaxpr/all_to_all | solution.py:10
  406.5 8.9 %all-to-all-done = bf16[32,32,256]{2,1,0:T(8,128)(2,1)S(1)} async-done(((bf16[32,32,256]{2,1,0:T(8,128)(2,1)}), bf16[32,32,256]{2,1,0:T(8,128)(2,1)S(1)}, u32[]{:S(2)}, u32[]{:S(2)}) %all-to-all-start) | async-done | bytes 524320 | tf_op jit(solution)/shard_map/while/body/eval_jaxpr/all_to_all | solution.py:10
  426.1 27.2 %psum.14 = bf16[2,32,256]{2,1,0:T(8,128)(2,1)S(1)} all-reduce(bf16[2,32,256]{2,1,0:T(8,128)(2,1)S(1)} %broadcast_select_fusion), channel_id=1, replica_groups=mesh['section'=8,'tp'=32] {'section'}, use_global_device_ids=true, to_apply=%region_3.4 | all-reduce | flops 16384 | bytes 65536 | tf_op jit(solution)/shard_map/psum | solution.py:22
  453.5 79.3 %psum.15 = f32[8,256]{1,0:T(8,128)S(1)} all-reduce(f32[8,256]{1,0:T(8,128)S(1)} %fusion.5), channel_id=1, replica_groups=mesh['section'=8,'tp'=32] {'tp'}, use_global_device_ids=true, to_apply=%region_4.5 | all-reduce | flops 2048 | bytes 16384 | tf_op jit(solution)/shard_map/psum | solution.py:65
  (108 shorter events, 138.4 us)
Async XLA Ops:
  0.6 452.7 %copy-start = (bf16[256,256]{1,0:T(8,128)(2,1)S(1)}, bf16[256,256]{1,0:T(8,128)(2,1)}, u32[]{:S(2)}) copy-start(bf16[256,256]{1,0:T(8,128)(2,1)} %param.11) | copy-start | bytes 393220
  62.5 15.0 %copy-start.3 = (s32[2,4]{1,0:T(2,128)S(1)}, s32[2,4]{1,0:T(2,128)}, u32[]{:S(2)}) copy-start(s32[2,4]{1,0:T(2,128)} %param.13) | copy-start | bytes 100
  69.5 58.7 %all-to-all-start.1 = ((bf16[32,2,32768]{2,1,0:T(2,128)(2,1)}), bf16[32,2,32768]{2,1,0:T(2,128)(2,1)}, u32[]{:S(2)}, u32[]{:S(2)}) async-start(bf16[32,2,32768]{2,1,0:T(2,128)(2,1)} %reshape.71), calls=%async_computation.1 | async-start | bytes 8388608 | tf_op jit(solution)/shard_map/all_to_all | solution.py:26
  178.0 7.5 %copy-start.1 = (bf16[2,32,256]{2,1,0:T(8,128)(2,1)S(1)}, bf16[2,32,256]{2,1,0:T(8,128)(2,1)}, u32[]{:S(2)}) copy-start(bf16[2,32,256]{2,1,0:T(8,128)(2,1)} %param.8) | copy-start | bytes 98308
  185.6 348.1 %copy-start.2 = (f32[2,4]{1,0:T(2,128)S(1)}, f32[2,4]{1,0:T(2,128)}, u32[]{:S(2)}) copy-start(f32[2,4]{1,0:T(2,128)} %param.12) | copy-start | bytes 100
  186.5 21.9 %all-to-all-start = ((bf16[32,32,256]{2,1,0:T(8,128)(2,1)}), bf16[32,32,256]{2,1,0:T(8,128)(2,1)S(1)}, u32[]{:S(2)}, u32[]{:S(2)}) async-start(bf16[32,32,256]{2,1,0:T(8,128)(2,1)} %stack.7), calls=%async_computation | async-start | bytes 1048576 | tf_op jit(solution)/shard_map/while/body/eval_jaxpr/all_to_all | solution.py:10
  211.9 7.2 %collective-permute-start = (bf16[32,256]{1,0:T(8,128)(2,1)S(1)}, bf16[32,256]{1,0:T(8,128)(2,1)S(1)}, u32[]{:S(2)}, u32[]{:S(2)}) collective-permute-start(bf16[32,256]{1,0:T(8,128)(2,1)S(1)} %get-tuple-element.227), channel_id=1, source_target_pairs={{0,32},{32,64},{64,96},{96,128},{128,160},{160,192},{192,224},{1,3... | collective-permute-start | bytes 49160 | tf_op jit(solution)/shard_map/while/body/eval_jaxpr/ppermute | solution.py:17
  219.9 14.3 %all-to-all-start = ((bf16[32,32,256]{2,1,0:T(8,128)(2,1)}), bf16[32,32,256]{2,1,0:T(8,128)(2,1)S(1)}, u32[]{:S(2)}, u32[]{:S(2)}) async-start(bf16[32,32,256]{2,1,0:T(8,128)(2,1)} %stack.7), calls=%async_computation | async-start | bytes 1048576 | tf_op jit(solution)/shard_map/while/body/eval_jaxpr/all_to_all | solution.py:10
  237.8 7.2 %collective-permute-start = (bf16[32,256]{1,0:T(8,128)(2,1)S(1)}, bf16[32,256]{1,0:T(8,128)(2,1)S(1)}, u32[]{:S(2)}, u32[]{:S(2)}) collective-permute-start(bf16[32,256]{1,0:T(8,128)(2,1)S(1)} %get-tuple-element.227), channel_id=1, source_target_pairs={{0,32},{32,64},{64,96},{96,128},{128,160},{160,192},{192,224},{1,3... | collective-permute-start | bytes 49160 | tf_op jit(solution)/shard_map/while/body/eval_jaxpr/ppermute | solution.py:17
  245.8 14.3 %all-to-all-start = ((bf16[32,32,256]{2,1,0:T(8,128)(2,1)}), bf16[32,32,256]{2,1,0:T(8,128)(2,1)S(1)}, u32[]{:S(2)}, u32[]{:S(2)}) async-start(bf16[32,32,256]{2,1,0:T(8,128)(2,1)} %stack.7), calls=%async_computation | async-start | bytes 1048576 | tf_op jit(solution)/shard_map/while/body/eval_jaxpr/all_to_all | solution.py:10
  263.6 7.2 %collective-permute-start = (bf16[32,256]{1,0:T(8,128)(2,1)S(1)}, bf16[32,256]{1,0:T(8,128)(2,1)S(1)}, u32[]{:S(2)}, u32[]{:S(2)}) collective-permute-start(bf16[32,256]{1,0:T(8,128)(2,1)S(1)} %get-tuple-element.227), channel_id=1, source_target_pairs={{0,32},{32,64},{64,96},{96,128},{128,160},{160,192},{192,224},{1,3... | collective-permute-start | bytes 49160 | tf_op jit(solution)/shard_map/while/body/eval_jaxpr/ppermute | solution.py:17
  271.7 14.3 %all-to-all-start = ((bf16[32,32,256]{2,1,0:T(8,128)(2,1)}), bf16[32,32,256]{2,1,0:T(8,128)(2,1)S(1)}, u32[]{:S(2)}, u32[]{:S(2)}) async-start(bf16[32,32,256]{2,1,0:T(8,128)(2,1)} %stack.7), calls=%async_computation | async-start | bytes 1048576 | tf_op jit(solution)/shard_map/while/body/eval_jaxpr/all_to_all | solution.py:10
  289.5 7.2 %collective-permute-start = (bf16[32,256]{1,0:T(8,128)(2,1)S(1)}, bf16[32,256]{1,0:T(8,128)(2,1)S(1)}, u32[]{:S(2)}, u32[]{:S(2)}) collective-permute-start(bf16[32,256]{1,0:T(8,128)(2,1)S(1)} %get-tuple-element.227), channel_id=1, source_target_pairs={{0,32},{32,64},{64,96},{96,128},{128,160},{160,192},{192,224},{1,3... | collective-permute-start | bytes 49160 | tf_op jit(solution)/shard_map/while/body/eval_jaxpr/ppermute | solution.py:17
  297.6 14.3 %all-to-all-start = ((bf16[32,32,256]{2,1,0:T(8,128)(2,1)}), bf16[32,32,256]{2,1,0:T(8,128)(2,1)S(1)}, u32[]{:S(2)}, u32[]{:S(2)}) async-start(bf16[32,32,256]{2,1,0:T(8,128)(2,1)} %stack.7), calls=%async_computation | async-start | bytes 1048576 | tf_op jit(solution)/shard_map/while/body/eval_jaxpr/all_to_all | solution.py:10
  315.4 7.2 %collective-permute-start = (bf16[32,256]{1,0:T(8,128)(2,1)S(1)}, bf16[32,256]{1,0:T(8,128)(2,1)S(1)}, u32[]{:S(2)}, u32[]{:S(2)}) collective-permute-start(bf16[32,256]{1,0:T(8,128)(2,1)S(1)} %get-tuple-element.227), channel_id=1, source_target_pairs={{0,32},{32,64},{64,96},{96,128},{128,160},{160,192},{192,224},{1,3... | collective-permute-start | bytes 49160 | tf_op jit(solution)/shard_map/while/body/eval_jaxpr/ppermute | solution.py:17
  323.4 14.3 %all-to-all-start = ((bf16[32,32,256]{2,1,0:T(8,128)(2,1)}), bf16[32,32,256]{2,1,0:T(8,128)(2,1)S(1)}, u32[]{:S(2)}, u32[]{:S(2)}) async-start(bf16[32,32,256]{2,1,0:T(8,128)(2,1)} %stack.7), calls=%async_computation | async-start | bytes 1048576 | tf_op jit(solution)/shard_map/while/body/eval_jaxpr/all_to_all | solution.py:10
  341.3 7.2 %collective-permute-start = (bf16[32,256]{1,0:T(8,128)(2,1)S(1)}, bf16[32,256]{1,0:T(8,128)(2,1)S(1)}, u32[]{:S(2)}, u32[]{:S(2)}) collective-permute-start(bf16[32,256]{1,0:T(8,128)(2,1)S(1)} %get-tuple-element.227), channel_id=1, source_target_pairs={{0,32},{32,64},{64,96},{96,128},{128,160},{160,192},{192,224},{1,3... | collective-permute-start | bytes 49160 | tf_op jit(solution)/shard_map/while/body/eval_jaxpr/ppermute | solution.py:17
  349.3 14.3 %all-to-all-start = ((bf16[32,32,256]{2,1,0:T(8,128)(2,1)}), bf16[32,32,256]{2,1,0:T(8,128)(2,1)S(1)}, u32[]{:S(2)}, u32[]{:S(2)}) async-start(bf16[32,32,256]{2,1,0:T(8,128)(2,1)} %stack.7), calls=%async_computation | async-start | bytes 1048576 | tf_op jit(solution)/shard_map/while/body/eval_jaxpr/all_to_all | solution.py:10
  367.2 7.2 %collective-permute-start = (bf16[32,256]{1,0:T(8,128)(2,1)S(1)}, bf16[32,256]{1,0:T(8,128)(2,1)S(1)}, u32[]{:S(2)}, u32[]{:S(2)}) collective-permute-start(bf16[32,256]{1,0:T(8,128)(2,1)S(1)} %get-tuple-element.227), channel_id=1, source_target_pairs={{0,32},{32,64},{64,96},{96,128},{128,160},{160,192},{192,224},{1,3... | collective-permute-start | bytes 49160 | tf_op jit(solution)/shard_map/while/body/eval_jaxpr/ppermute | solution.py:17
  375.2 14.3 %all-to-all-start = ((bf16[32,32,256]{2,1,0:T(8,128)(2,1)}), bf16[32,32,256]{2,1,0:T(8,128)(2,1)S(1)}, u32[]{:S(2)}, u32[]{:S(2)}) async-start(bf16[32,32,256]{2,1,0:T(8,128)(2,1)} %stack.7), calls=%async_computation | async-start | bytes 1048576 | tf_op jit(solution)/shard_map/while/body/eval_jaxpr/all_to_all | solution.py:10
  393.0 7.2 %collective-permute-start = (bf16[32,256]{1,0:T(8,128)(2,1)S(1)}, bf16[32,256]{1,0:T(8,128)(2,1)S(1)}, u32[]{:S(2)}, u32[]{:S(2)}) collective-permute-start(bf16[32,256]{1,0:T(8,128)(2,1)S(1)} %get-tuple-element.227), channel_id=1, source_target_pairs={{0,32},{32,64},{64,96},{96,128},{128,160},{160,192},{192,224},{1,3... | collective-permute-start | bytes 49160 | tf_op jit(solution)/shard_map/while/body/eval_jaxpr/ppermute | solution.py:17
  401.1 14.3 %all-to-all-start = ((bf16[32,32,256]{2,1,0:T(8,128)(2,1)}), bf16[32,32,256]{2,1,0:T(8,128)(2,1)S(1)}, u32[]{:S(2)}, u32[]{:S(2)}) async-start(bf16[32,32,256]{2,1,0:T(8,128)(2,1)} %stack.7), calls=%async_computation | async-start | bytes 1048576 | tf_op jit(solution)/shard_map/while/body/eval_jaxpr/all_to_all | solution.py:10
  418.9 7.2 %collective-permute-start = (bf16[32,256]{1,0:T(8,128)(2,1)S(1)}, bf16[32,256]{1,0:T(8,128)(2,1)S(1)}, u32[]{:S(2)}, u32[]{:S(2)}) collective-permute-start(bf16[32,256]{1,0:T(8,128)(2,1)S(1)} %get-tuple-element.227), channel_id=1, source_target_pairs={{0,32},{32,64},{64,96},{96,128},{128,160},{160,192},{192,224},{1,3... | collective-permute-start | bytes 49160 | tf_op jit(solution)/shard_map/while/body/eval_jaxpr/ppermute | solution.py:17
